TPU v7x, 256 devices: a whole 4x4x8 slice. The times are simulated.
256 devices in a mesh: dom: 32 (over x, z), grp: 8 (over y, core).
Axes of the slice: x: 4, y: 4, z: 8, core: 2. Of those that a mesh axis runs over, the one named last changes fastest.
Arguments:
- node_feats: bfloat16 [65536, 1024], P(('dom', 'grp')), may hold values from -6 to 6
- weight: bfloat16 [1024, 512], replicated, may hold values from -0.1875 to 0.1875
- bias: float32 [512], replicated, may hold values from -4 to 4
- cotangent: bfloat16 [65536, 512], P(('dom', 'grp')), may hold values from -6 to 6
- tile_bank: bfloat16 [16, 128, 128], replicated, may hold values from -0.125 to 0.125
- local_cols: int32 [32, 16, 16], P('dom'), may hold values from 0 to 15
- local_banks: int32 [32, 16, 16], P('dom'), may hold values from 0 to 15
- published: int32 [32, 4], P('dom'), may hold values from 0 to 15, as said below
- send_table: int32 [32, 32, 2], replicated, may hold values from -1 to 3, as said below
- halo_rows: int32 [32, 32, 2], P('dom'), may hold values from 0 to 15
- halo_banks: int32 [32, 32, 2], P('dom'), may hold values from 0 to 15
Outputs:
- activations: bfloat16 [65536, 512], P(('dom', 'grp'))
- grad_nodes: bfloat16 [65536, 1024], P(('dom', 'grp'))
- grad_weight: float32 [1024, 512], replicated
- grad_bias: float32 [512], replicated
Inputs may be any that keep to these rules, and one draw needn't show every extreme that they name: `published`: the 4 entries of a partition are distinct block numbers of that partition; 0 and 15 each appear in some partition's list. `send_table`: entry s of the pair (src, p) is -1 or an index into the offered list of src; the live entries of a pair come first and are distinct; a pair (p, p) has none; some pair has all 2 entries live.
All inputs are finite; a program needn't handle non-finite values.
Results may differ from a plain program's by a relative error of at most 0.019.
The roundings to bfloat16 on the way count: a program that leaves them out, or rounds other values in their place, can miss the bound.
Values may be sent and summed in bfloat16 or wider, within the bound.
A program may use at most 64 MiB of HBM per device.

v0:
```python
import jax
import jax.numpy as jnp
from jax import lax
from jax.sharding import PartitionSpec as P


def per_device(
    node_feats,
    weight,
    bias,
    cotangent,
    tile_bank,
    local_cols,
    local_banks,
    published,
    send_table,
    halo_rows,
    halo_banks,
):
    domains = lax.axis_size("dom")
    groups = lax.axis_size("grp")
    domain_index = lax.axis_index("dom")
    rows_here = node_feats.shape[0]
    tile_size = tile_bank.shape[1]
    slot_count = send_table.shape[2]
    pub_count = published.shape[1]
    tiles_row = local_cols.shape[2]
    features = lax.all_to_all(node_feats, "grp", split_axis=1, concat_axis=0, tiled=True)
    part_rows, narrow = features.shape
    blocks = part_rows // tile_size
    feat_blocks = features.reshape(blocks, tile_size, narrow)
    cols_here = local_cols[0]
    banks_here = local_banks[0]
    own_pub = published[0]
    incoming = lax.dynamic_index_in_dim(send_table, domain_index, 1, keepdims=False)
    live_in = (incoming >= 0).astype(jnp.float32)[:, :, None, None]
    rows_in = halo_rows[0]
    halo_tiles = tile_bank[halo_banks[0]]
    source_ids = lax.broadcasted_iota(jnp.int32, (domains, slot_count), 0)
    gathered_ids = source_ids * pub_count + jnp.maximum(incoming, 0)

    def forward_tiles(position, running):
        column = lax.dynamic_index_in_dim(cols_here, position, 1, keepdims=False)
        bank_ids = lax.dynamic_index_in_dim(banks_here, position, 1, keepdims=False)
        return running + jnp.einsum(
            "rij,rjf->rif",
            tile_bank[bank_ids],
            feat_blocks[column],
            preferred_element_type=jnp.float32,
        )

    running = lax.fori_loop(
        0, tiles_row, forward_tiles, jnp.zeros((blocks, tile_size, narrow), jnp.float32)
    )
    shared = feat_blocks[own_pub]
    everyone = lax.all_gather(shared, "dom", axis=0, tiled=True)
    remote = everyone[gathered_ids]
    halo_terms = (
        jnp.einsum("dsij,dsjf->dsif", halo_tiles, remote, preferred_element_type=jnp.float32)
        * live_in
    )
    running = running + jax.ops.segment_sum(
        halo_terms.reshape(domains * slot_count, tile_size, narrow),
        rows_in.reshape(-1),
        num_segments=blocks,
    )
    agg_narrow = running.astype(jnp.bfloat16).reshape(part_rows, narrow)
    aggregated = lax.all_to_all(agg_narrow, "grp", split_axis=0, concat_axis=1, tiled=True)
    pre_act = jnp.dot(aggregated, weight, preferred_element_type=jnp.float32) + bias
    activations = jnp.maximum(pre_act, 0.0).astype(jnp.bfloat16)
    grad_pre = jnp.where(pre_act > 0, cotangent.astype(jnp.float32), 0.0).astype(jnp.bfloat16)
    weight_part = lax.dot_general(
        aggregated, grad_pre, (((0,), (0,)), ((), ())), preferred_element_type=jnp.float32
    )
    bias_part = jnp.sum(grad_pre.astype(jnp.float32), axis=0)
    grad_agg = lax.dot_general(
        grad_pre, weight, (((1,), (1,)), ((), ())), preferred_element_type=jnp.float32
    ).astype(jnp.bfloat16)
    grad_narrow = lax.all_to_all(grad_agg, "grp", split_axis=1, concat_axis=0, tiled=True)
    grad_blocks = grad_narrow.reshape(blocks, tile_size, narrow)

    def backward_tiles(position, running):
        column = lax.dynamic_index_in_dim(cols_here, position, 1, keepdims=False)
        bank_ids = lax.dynamic_index_in_dim(banks_here, position, 1, keepdims=False)
        contrib = jnp.einsum(
            "rji,rjf->rif", tile_bank[bank_ids], grad_blocks, preferred_element_type=jnp.float32
        )
        return running + jax.ops.segment_sum(contrib, column, num_segments=blocks)

    grad_total = lax.fori_loop(
        0, tiles_row, backward_tiles, jnp.zeros((blocks, tile_size, narrow), jnp.float32)
    )
    back_terms = (
        jnp.einsum(
            "dsji,dsjf->dsif", halo_tiles, grad_blocks[rows_in], preferred_element_type=jnp.float32
        )
        * live_in
    )
    placed = jax.ops.segment_sum(
        back_terms.reshape(domains * slot_count, tile_size, narrow),
        gathered_ids.reshape(-1),
        num_segments=domains * pub_count,
    )
    mine_back = lax.psum_scatter(placed, "dom", scatter_dimension=0, tiled=True)
    back_total = jax.ops.segment_sum(mine_back, own_pub, num_segments=blocks)
    grad_total = grad_total + back_total
    grad_nodes = lax.all_to_all(
        grad_total.astype(jnp.bfloat16).reshape(part_rows, narrow),
        "grp",
        split_axis=0,
        concat_axis=1,
        tiled=True,
    )
    norm_scale = float(rows_here * groups * domains) ** (-0.5)
    weight_total, bias_total = lax.psum((weight_part, bias_part), ("dom", "grp"))
    return (activations, grad_nodes, weight_total * norm_scale, bias_total * norm_scale)


def solution(mesh):
    in_specs = (
        P(("dom", "grp"), None),
        P(),
        P(),
        P(("dom", "grp"), None),
        P(),
        P("dom", None, None),
        P("dom", None, None),
        P("dom", None),
        P(),
        P("dom", None, None),
        P("dom", None, None),
    )
    out_specs = (P(("dom", "grp"), None), P(("dom", "grp"), None), P(), P())
    return jax.shard_map(
        per_device, mesh=mesh, in_specs=in_specs, out_specs=out_specs, check_vma=False
    )
```

profile of v0, /device:TPU:2, one launch (start us, length us, event | category | flops | bytes accessed | tf_op | source)
XLA Modules:
  0.0 686.9 jit_solution(15913844381797116386)
XLA Ops:
  7.2 2.0 copy_bitcast_fusion.1
  9.3 4.5 all-to-all-start
  14.9 2.1 gather_fusion.3
  17.1 7.1 %all-to-all-done = bf16[256,8,128]{2,0,1:T(8,128)(2,1)} async-done(((bf16[256,8,128]{2,0,1:T(8,128)(2,1)}), bf16[256,8,128]{2,0,1:T(8,128)(2,1)}, u32[]{:S(2)}, u32[]{:S(2)}) %all-to-all-start) | async-done | bytes 524320 | tf_op jit(solution)/shard_map/all_to_all | solution.py:28
  24.2 2.3 gather_fusion.4
  26.5 74.0 %while.28 = (s32[]{:T(128)}, f32[16,128,128]{2,1,0:T(8,128)S(1)}, s32[16,16]{0,1:T(8,128)S(1)}, bf16[16,128,128]{2,1,0:T(8,128)(2,1)S(1)}, s32[16,16]{0,1:T(8,12...) while((s32[]{:T(128)}, f32[16,128,128]{2,1,0:T(8,128)S(1)}, ...), condition=%wide.region_1.2_spmd.clone, body=%wide.region_0.1_spmd.clone.sunk | while | flops 67635296 | bytes 5251683 | solution.py:52
  27.2 2.4 gather_fusion.2
  31.8 2.4 gather_fusion.2
  36.4 2.4 gather_fusion.2
  38.9 1.5 convolution_add_fusion.3
  41.1 2.4 gather_fusion.2
  43.5 1.4 convolution_add_fusion.3
  45.7 2.5 gather_fusion.2
  48.2 1.4 convolution_add_fusion.3
  50.3 2.4 gather_fusion.2
  52.8 1.5 convolution_add_fusion.3
  55.0 2.4 gather_fusion.2
  59.6 2.4 gather_fusion.2
  64.2 2.4 gather_fusion.2
  68.8 2.4 gather_fusion.2
  73.4 2.4 gather_fusion.2
  78.1 2.4 gather_fusion.2
  82.7 2.5 gather_fusion.2
  87.3 2.4 gather_fusion.2
  91.9 2.5 gather_fusion.2
  96.6 2.4 gather_fusion.2
  99.0 1.5 convolution_add_fusion.3
  100.5 7.6 %all-gather.3.cloned.1.call-done = bf16[128,128,128]{2,1,0:T(8,128)(2,1)} async-done(((bf16[4,128,128]{2,1,0:T(8,128)(2,1)}), bf16[128,128,128]{2,1,0:T(8,128)(2,1)}) %all-gather.3.cloned.1.call-update) | async-done | bytes 4194320 | tf_op jit(solution)/shard_map/all_gather | solution.py:56
  108.1 4.3 gather_fusion.5
  112.4 4.9 convolution_multiply_fusion.1
  117.2 8.8 %scatter_fusion.1 = f32[16,128,128]{2,1,0:T(8,128)S(1)} fusion(f32[16,128,128]{2,1,0:T(8,128)S(1)} %get-tuple-element.222, s32[64]{0:T(128)S(1)} %reshape.272, f32[64,128,128]{2,1,0:T(8,128)} %bitcast.94), kind=kCustom, calls=%fused_computation.8 | custom fusion | flops 1048576 | bytes 12583168 | tf_op jit(solution)/shard_map/scatter-add | solution.py:62
  126.9 4.4 all-to-all-start.1
  131.6 10.1 %all-to-all-done.1 = bf16[8,256,128]{2,1,0:T(8,128)(2,1)S(1)} async-done(((bf16[8,256,128]{2,1,0:T(8,128)(2,1)}), bf16[8,256,128]{2,1,0:T(8,128)(2,1)S(1)}, u32[]{:S(2)}, u32[]{:S(2)}) %all-to-all-start.1) | async-done | bytes 524320 | tf_op jit(solution)/shard_map/all_to_all | solution.py:68
  144.6 3.5 all-to-all-start.2
  148.6 9.8 %all-to-all-done.2 = bf16[256,8,128]{2,0,1:T(8,128)(2,1)S(1)} async-done(((bf16[256,8,128]{2,0,1:T(8,128)(2,1)}), bf16[256,8,128]{2,0,1:T(8,128)(2,1)S(1)}, u32[]{:S(2)}, u32[]{:S(2)}) %all-to-all-start.2) | async-done | bytes 524320 | tf_op jit(solution)/shard_map/all_to_all | solution.py:79
  158.4 2.2 gather_fusion.6
  160.5 5.2 convolution_multiply_fusion
  165.8 4.3 broadcast_in_dim.12
  170.0 13.4 %scatter_fusion.2 = f32[128,128,128]{2,1,0:T(8,128)} fusion(f32[128,128,128]{2,1,0:T(8,128)} %broadcast_in_dim.12, s32[64]{0:T(128)S(1)} %add_bitcast_fusion, f32[64,128,128]{2,1,0:T(8,128)} %bitcast.93), kind=kCustom, calls=%fused_computation.9 | custom fusion | flops 1048576 | bytes 12583168 | tf_op jit(solution)/shard_map/scatter-add | solution.py:99
  183.5 75.8 %psum.15 = f32[512]{0:T(512)S(1)} all-reduce(f32[512]{0:T(512)S(1)} %get-tuple-element.277), channel_id=1, replica_groups=mesh['dom'=32,'grp'=8] {'dom','grp'}, use_global_device_ids=true, to_apply=%region_11.12 | all-reduce | flops 512 | bytes 4096 | tf_op jit(solution)/shard_map/psum | solution.py:115
  259.3 1.8 fusion.7
  262.2 98.2 %while.27 = (s32[]{:T(128)}, f32[16,128,128]{2,1,0:T(8,128)}, s32[16,16]{0,1:T(8,128)S(1)}, s32[16,16]{0,1:T(8,128)S(1)}, bf16[16,128,128]{2,1,0:T(8,128)(2,1)S(...) while((s32[]{:T(128)}, f32[16,128,128]{2,1,0:T(8,128)}, s32[16,16]{0,1:T(8,128)S(1)}, ...), condition=%wide.region_5.6_spmd, body=%wide.region_3.5_spmd.sunk | while | flops 67372080 | bytes 6296081 | solution.py:90
  265.0 3.3 scatter_fusion
  271.2 3.3 scatter_fusion
  277.3 3.3 scatter_fusion
  283.4 3.3 scatter_fusion
  289.6 3.3 scatter_fusion
  295.7 3.3 scatter_fusion
  301.9 3.3 scatter_fusion
  308.1 3.3 scatter_fusion
  314.2 3.3 scatter_fusion
  320.3 3.4 scatter_fusion
  326.5 3.3 scatter_fusion
  332.7 3.3 scatter_fusion
  338.8 3.3 scatter_fusion
  344.9 3.3 scatter_fusion
  351.0 3.3 scatter_fusion
  357.1 3.3 scatter_fusion
  360.4 48.2 %reduce-scatter.2.cloned.1.call-done = f32[4,128,128]{2,1,0:T(8,128)} async-done(((f32[128,128,128]{2,1,0:T(8,128)}), f32[4,128,128]{2,1,0:T(8,128)}) %reduce-scatter.2.cloned.1.call-update) | async-done | bytes 262160 | tf_op jit(solution)/shard_map/reduce_scatter | solution.py:104
  408.7 2.5 scatter_fusion.3
  411.1 2.1 convert_element_type.38
  413.3 4.3 all-to-all-start.3
  418.1 257.9 %all-reduce.2.cloned.1.call-done = f32[1024,512]{1,0:T(8,128)} async-done(((f32[1024,512]{1,0:T(8,128)}), f32[1024,512]{1,0:T(8,128)}) %all-reduce.2.cloned.1.call-update) | async-done | bytes 2097168 | tf_op jit(solution)/shard_map/psum | solution.py:115
  676.0 3.1 broadcast_multiply_fusion
  (206 shorter events, 80.1 us)
Async XLA Ops:
  7.2 134.8 %copy-start = (bf16[1024,512]{1,0:T(8,128)(2,1)S(1)}, bf16[1024,512]{1,0:T(8,128)(2,1)}, u32[]{:S(2)}) copy-start(bf16[1024,512]{1,0:T(8,128)(2,1)} %param.16) | copy-start | bytes 3145732
  7.2 6.6 copy-start.3
  7.2 6.8 copy-start.8
  7.2 7.4 %copy-start.4 = (s32[1,16,16]{2,1,0:T(8,128)S(1)}, s32[1,16,16]{2,1,0:T(8,128)}, u32[]{:S(2)}) copy-start(s32[1,16,16]{2,1,0:T(8,128)} %param.21) | copy-start | bytes 3076
  7.2 7.4 %copy-start.5 = (s32[1,16,16]{2,1,0:T(8,128)S(1)}, s32[1,16,16]{2,1,0:T(8,128)}, u32[]{:S(2)}) copy-start(s32[1,16,16]{2,1,0:T(8,128)} %param.20) | copy-start | bytes 3076
  7.2 7.5 %copy-start.6 = (s32[1,32,2]{1,2,0:T(2,128)S(1)}, s32[1,32,2]{1,2,0:T(2,128)}, u32[]{:S(2)}) copy-start(s32[1,32,2]{1,2,0:T(2,128)} %param.24) | copy-start | bytes 772
  7.2 7.7 %copy-start.1 = (bf16[16,128,128]{2,1,0:T(8,128)(2,1)S(1)}, bf16[16,128,128]{2,1,0:T(8,128)(2,1)}, u32[]{:S(2)}) copy-start(bf16[16,128,128]{2,1,0:T(8,128)(2,1)} %param.19) | copy-start | bytes 1572868
  9.3 14.9 %all-to-all-start = ((bf16[256,8,128]{2,0,1:T(8,128)(2,1)}), bf16[256,8,128]{2,0,1:T(8,128)(2,1)}, u32[]{:S(2)}, u32[]{:S(2)}) async-start(bf16[256,8,128]{2,0,1:T(8,128)(2,1)} %copy_bitcast_fusion.1), calls=%async_computation | async-start | bytes 1048576 | tf_op jit(solution)/shard_map/all_to_all | solution.py:28
  13.8 94.3 %all-gather.3.cloned.1.call-start = ((), (), s32[]{:S(2)}) async-start(), calls=%async_computation.7 | async-start | bytes 4325376 | tf_op jit(solution)/shard_map/all_gather | solution.py:56
  14.9 2.2 copy-start.9
  126.0 15.9 %copy-start.7 = (f32[512]{0:T(512)S(1)}, f32[512]{0:T(512)}, u32[]{:S(2)}) copy-start(f32[512]{0:T(512)} %param.17) | copy-start | bytes 6148
  126.9 16.2 %copy-start.2 = (bf16[256,512]{1,0:T(8,128)(2,1)S(1)}, bf16[256,512]{1,0:T(8,128)(2,1)}, u32[]{:S(2)}) copy-start(bf16[256,512]{1,0:T(8,128)(2,1)} %param.18) | copy-start | bytes 786436
  126.9 14.8 %all-to-all-start.1 = ((bf16[8,256,128]{2,1,0:T(8,128)(2,1)}), bf16[8,256,128]{2,1,0:T(8,128)(2,1)S(1)}, u32[]{:S(2)}, u32[]{:S(2)}) async-start(bf16[8,256,128]{2,1,0:T(8,128)(2,1)} %bitcast.15), calls=%async_computation.1 | async-start | bytes 1048576 | tf_op jit(solution)/shard_map/all_to_all | solution.py:68
  144.6 13.8 %all-to-all-start.2 = ((bf16[256,8,128]{2,0,1:T(8,128)(2,1)}), bf16[256,8,128]{2,0,1:T(8,128)(2,1)S(1)}, u32[]{:S(2)}, u32[]{:S(2)}) async-start(bf16[256,8,128]{2,0,1:T(8,128)(2,1)} %bitcast.76), calls=%async_computation.2 | async-start | bytes 1048576 | tf_op jit(solution)/shard_map/all_to_all | solution.py:79
  148.1 260.6 %reduce-scatter.2.cloned.1.call-start = ((), (), s32[]{:S(2)}) async-start(), calls=%async_computation.5 | async-start | bytes 8650752 | tf_op jit(solution)/shard_map/reduce_scatter | solution.py:104
  183.5 492.5 %all-reduce.2.cloned.1.call-start = ((), (), s32[]{:S(2)}) async-start(), calls=%async_computation.6 | async-start | bytes 4194304 | tf_op jit(solution)/shard_map/psum | solution.py:115
  413.3 265.9 %all-to-all-start.3 = ((bf16[8,256,128]{2,1,0:T(8,128)(2,1)}), bf16[8,256,128]{2,1,0:T(8,128)(2,1)S(1)}, u32[]{:S(2)}, u32[]{:S(2)}) async-start(bf16[8,256,128]{2,1,0:T(8,128)(2,1)} %bitcast.26), calls=%async_computation.4 | async-start | bytes 1048576 | tf_op jit(solution)/shard_map/all_to_all | solution.py:107
Sparse Core Ops, SparseCore 0:
  26.6 81.3 all-gather.2
  183.6 225.0 reduce-scatter.1
  415.5 260.4 all-reduce.1
where the time goes:
time: 691 us; the launch traced here: 687 us
  waiting for transfers between devices  341 us (49%)
  local copies, waits for them, and re-layouts  94.3 us (14%)
  other arithmetic  85.3 us (12%)
  blocking collectives  75.8 us (11%)
  matrix products  58.9 us (9%)
  starting transfers between devices  16.8 us (2%)
  between operations  14 us (2%)
    psum x1, waiting for transfers between devices, per_device(): lax.psum((weight_part, bias_part), ('dom', 'grp'))  258 us
    psum x1, blocking collectives, per_device(): lax.psum((weight_part, bias_part), ('dom', 'grp'))  75.8 us
    scatter-add x16, other arithmetic, backward_tiles(): return running + jax.ops.segment_sum(contrib, column, num_segments=blocks)  53.1 us
    reduce_scatter x1, waiting for transfers between devices, per_device(): mine_back = lax.psum_scatter(placed, 'dom', scatter_dimension=0, tiled=True)  48.2 us
    gather x16, local copies, waits for them, and re-layouts, forward_tiles(): feat_blocks[column]  39.2 us
    dot_general x16, matrix products, forward_tiles(): jnp.einsum('rij,rjf->rif', tile_bank[bank_ids], feat_blocks[column], pref...  23.2 us
    gather x16, local copies, waits for them, and re-layouts, backward_tiles(): tile_bank[bank_ids]  22.5 us
    dot_general x16, matrix products, backward_tiles(): jnp.einsum('rji,rjf->rif', tile_bank[bank_ids], grad_blocks, preferred_el...  22.3 us
  transfers between devices with their start and end apart: 7, of which 6 were waited for; matrix products, arithmetic and copies ran while one was open for 27% of the time, Pallas kernels for 0%

commit v1 on v0

--- a/solution.py
+++ b/solution.py
@@ -1,7 +1,16 @@
+import functools
 import jax
 import jax.numpy as jnp
 from jax import lax
 from jax.sharding import PartitionSpec as P
+from jax.lax import psum
+
+
+def _render_strings(inp, axis_id, row_axis):
+    return psum(psum(inp, axis_id), row_axis)
+
+
+lift_rounds_here = functools.partial(_render_strings, axis_id="dom", row_axis="grp")
 
 
 def per_device(
@@ -112,7 +121,7 @@
         tiled=True,
     )
     norm_scale = float(rows_here * groups * domains) ** (-0.5)
-    weight_total, bias_total = lax.psum((weight_part, bias_part), ("dom", "grp"))
+    weight_total, bias_total = lift_rounds_here((weight_part, bias_part))
     return (activations, grad_nodes, weight_total * norm_scale, bias_total * norm_scale)
 
 

time: 691 us -> 614 us (0.89)
  waiting for transfers between devices: 341 us -> 254 us
  blocking collectives: 75.8 us -> 91 us
    psum x1 -> x2, waiting for transfers between devices: 258 us -> 97.5 us  [_render_strings(): return psum(psum(inp, axis_id), row_axis)]
    reduce_scatter x1, waiting for transfers between devices: 48.2 us -> 132 us  [per_device(): mine_back = lax.psum_scatter(placed, 'dom', scatter_dimension=0, tiled=True)]
    all_to_all x0 -> x1, blocking collectives: none -> 14.6 us  [per_device(): lax.all_to_all(agg_narrow, 'grp', split_axis=0, concat_axis=1, tiled=True)]
    all_to_all x1 -> x0, waiting for transfers between devices: 10.1 us -> none  [per_device(): lax.all_to_all(agg_narrow, 'grp', split_axis=0, concat_axis=1, tiled=True)]
    psum x1 -> x2, blocking collectives: 75.8 us -> 76.4 us  [_render_strings(): return psum(psum(inp, axis_id), row_axis)]
  transfers between devices with their start and end apart: 7 -> 7, of which waited for: 6 -> 6; matrix products, arithmetic and copies ran while one was open for 27% -> 34% of each run, Pallas kernels for 0% -> 0%
where the time goes in v1:
time: 614 us; the launch traced here: 610 us
  waiting for transfers between devices  254 us (41%)
  local copies, waits for them, and re-layouts  94.2 us (15%)
  blocking collectives  91 us (15%)
  other arithmetic  84.1 us (14%)
  matrix products  59 us (10%)
  between operations  14.1 us (2%)
  starting transfers between devices  12.4 us (2%)
    reduce_scatter x1, waiting for transfers between devices, per_device(): mine_back = lax.psum_scatter(placed, 'dom', scatter_dimension=0, tiled=True)  132 us
    psum x2, waiting for transfers between devices, _render_strings(): return psum(psum(inp, axis_id), row_axis)  97.5 us
    psum x2, blocking collectives, _render_strings(): return psum(psum(inp, axis_id), row_axis)  76.4 us
    scatter-add x16, other arithmetic, backward_tiles(): return running + jax.ops.segment_sum(contrib, column, num_segments=blocks)  52.7 us
    gather x16, local copies, waits for them, and re-layouts, forward_tiles(): feat_blocks[column]  39.2 us
    dot_general x16, matrix products, forward_tiles(): jnp.einsum('rij,rjf->rif', tile_bank[bank_ids], feat_blocks[column], pref...  23.2 us
    gather x16, local copies, waits for them, and re-layouts, backward_tiles(): tile_bank[bank_ids]  22.5 us
    dot_general x16, matrix products, backward_tiles(): jnp.einsum('rji,rjf->rif', tile_bank[bank_ids], grad_blocks, preferred_el...  22.3 us
  transfers between devices with their start and end apart: 7, of which 6 were waited for; matrix products, arithmetic and copies ran while one was open for 34% of the time, Pallas kernels for 0%

profile of v1, /device:TPU:2, one launch (start us, length us, event | category | flops | bytes accessed | tf_op | source)
XLA Modules:
  0.0 610.0 jit_solution(2101844328220292870)
XLA Ops:
  7.2 2.0 copy_bitcast_fusion.1
  9.3 4.5 all-to-all-start
  14.9 2.1 gather_fusion.3
  17.1 7.1 %all-to-all-done = bf16[256,8,128]{2,0,1:T(8,128)(2,1)} async-done(((bf16[256,8,128]{2,0,1:T(8,128)(2,1)}), bf16[256,8,128]{2,0,1:T(8,128)(2,1)}, u32[]{:S(2)}, u32[]{:S(2)}) %all-to-all-start) | async-done | bytes 524320 | tf_op jit(solution)/shard_map/all_to_all | solution.py:37
  24.2 2.3 gather_fusion.4
  26.5 74.0 %while.28 = (s32[]{:T(128)}, f32[16,128,128]{2,1,0:T(8,128)S(1)}, s32[16,16]{0,1:T(8,128)S(1)}, bf16[16,128,128]{2,1,0:T(8,128)(2,1)S(1)}, s32[16,16]{0,1:T(8,12...) while((s32[]{:T(128)}, f32[16,128,128]{2,1,0:T(8,128)S(1)}, ...), condition=%wide.region_1.2_spmd.clone, body=%wide.region_0.1_spmd.clone.sunk | while | flops 67635296 | bytes 5251683 | solution.py:61
  27.3 2.4 gather_fusion.2
  31.9 2.4 gather_fusion.2
  36.5 2.4 gather_fusion.2
  38.9 1.5 convolution_add_fusion.3
  41.1 2.4 gather_fusion.2
  43.6 1.4 convolution_add_fusion.3
  45.7 2.5 gather_fusion.2
  50.4 2.4 gather_fusion.2
  52.8 1.5 convolution_add_fusion.3
  55.0 2.4 gather_fusion.2
  59.6 2.4 gather_fusion.2
  64.2 2.4 gather_fusion.2
  68.9 2.4 gather_fusion.2
  73.5 2.4 gather_fusion.2
  78.1 2.4 gather_fusion.2
  82.7 2.5 gather_fusion.2
  87.4 2.4 gather_fusion.2
  92.0 2.5 gather_fusion.2
  96.6 2.4 gather_fusion.2
  99.1 1.5 convolution_add_fusion.3
  100.5 7.5 %all-gather.3.cloned.1.call-done = bf16[128,128,128]{2,1,0:T(8,128)(2,1)} async-done(((bf16[4,128,128]{2,1,0:T(8,128)(2,1)}), bf16[128,128,128]{2,1,0:T(8,128)(2,1)}) %all-gather.3.cloned.1.call-update) | async-done | bytes 4194320 | tf_op jit(solution)/shard_map/all_gather | solution.py:65
  108.1 4.3 gather_fusion.5
  112.4 4.9 convolution_multiply_fusion.1
  117.2 8.8 %scatter_fusion.1 = f32[16,128,128]{2,1,0:T(8,128)S(1)} fusion(f32[16,128,128]{2,1,0:T(8,128)S(1)} %get-tuple-element.222, s32[64]{0:T(128)S(1)} %reshape.272, f32[64,128,128]{2,1,0:T(8,128)} %bitcast.94), kind=kCustom, calls=%fused_computation.8 | custom fusion | flops 1048576 | bytes 12583168 | tf_op jit(solution)/shard_map/scatter-add | solution.py:71
  126.2 14.6 %all_to_all.70 = bf16[8,256,128]{2,1,0:T(8,128)(2,1)S(1)} all-to-all(bf16[8,256,128]{2,1,0:T(8,128)(2,1)S(1)} %bitcast.99), channel_id=1, replica_groups=mesh['dom'=32,'grp'=8] {'grp'}, dimensions={0} | all-to-all | bytes 1048576 | tf_op jit(solution)/shard_map/all_to_all | solution.py:77
  142.3 1.7 fusion.7
  145.6 3.5 all-to-all-start.2
  149.6 9.8 %all-to-all-done.2 = bf16[256,8,128]{2,0,1:T(8,128)(2,1)S(1)} async-done(((bf16[256,8,128]{2,0,1:T(8,128)(2,1)}), bf16[256,8,128]{2,0,1:T(8,128)(2,1)S(1)}, u32[]{:S(2)}, u32[]{:S(2)}) %all-to-all-start.2) | async-done | bytes 524320 | tf_op jit(solution)/shard_map/all_to_all | solution.py:88
  159.4 2.1 gather_fusion.6
  161.6 5.3 convolution_multiply_fusion
  166.8 4.3 broadcast_in_dim.12
  171.1 13.4 %scatter_fusion.2 = f32[128,128,128]{2,1,0:T(8,128)} fusion(f32[128,128,128]{2,1,0:T(8,128)} %broadcast_in_dim.12, s32[64]{0:T(128)S(1)} %add_bitcast_fusion, f32[64,128,128]{2,1,0:T(8,128)} %bitcast.93), kind=kCustom, calls=%fused_computation.9 | custom fusion | flops 1048576 | bytes 12583168 | tf_op jit(solution)/shard_map/scatter-add | solution.py:108
  184.6 63.9 %psum.30 = f32[512]{0:T(512)S(1)} all-reduce(f32[512]{0:T(512)S(1)} %get-tuple-element.277), channel_id=1, replica_groups=mesh['dom'=32,'grp'=8] {'dom'}, use_global_device_ids=true, to_apply=%region_12.13 | all-reduce | flops 512 | bytes 4096 | tf_op jit(solution)/shard_map/psum | solution.py:10
  248.5 12.4 %psum.31 = f32[512]{0:T(512)S(1)} all-reduce(f32[512]{0:T(512)S(1)} %psum.30), channel_id=1, replica_groups=mesh['dom'=32,'grp'=8] {'grp'}, use_global_device_ids=true, to_apply=%region_13.14 | all-reduce | flops 512 | bytes 4096 | tf_op jit(solution)/shard_map/psum | solution.py:10
  261.0 32.8 %all-reduce.3.cloned.1.call-done = f32[1024,512]{1,0:T(8,128)} async-done(((f32[1024,512]{1,0:T(8,128)}), f32[1024,512]{1,0:T(8,128)}) %all-reduce.3.cloned.1.call-update) | async-done | bytes 2097168 | tf_op jit(solution)/shard_map/psum | solution.py:10
  294.8 97.9 %while.27 = (s32[]{:T(128)}, f32[16,128,128]{2,1,0:T(8,128)}, s32[16,16]{0,1:T(8,128)S(1)}, s32[16,16]{0,1:T(8,128)S(1)}, bf16[16,128,128]{2,1,0:T(8,128)(2,1)S(...) while((s32[]{:T(128)}, f32[16,128,128]{2,1,0:T(8,128)}, s32[16,16]{0,1:T(8,128)S(1)}, ...), condition=%wide.region_5.6_spmd, body=%wide.region_3.5_spmd.sunk | while | flops 67372080 | bytes 6296081 | solution.py:99
  297.7 3.3 scatter_fusion
  303.8 3.2 scatter_fusion
  309.9 3.3 scatter_fusion
  316.0 3.3 scatter_fusion
  322.1 3.3 scatter_fusion
  328.2 3.3 scatter_fusion
  334.3 3.3 scatter_fusion
  340.4 3.3 scatter_fusion
  346.6 3.3 scatter_fusion
  352.7 3.3 scatter_fusion
  358.8 3.3 scatter_fusion
  365.0 3.3 scatter_fusion
  371.1 3.3 scatter_fusion
  377.2 3.3 scatter_fusion
  383.3 3.3 scatter_fusion
  389.4 3.3 scatter_fusion
  392.7 132.2 %reduce-scatter.2.cloned.1.call-done = f32[4,128,128]{2,1,0:T(8,128)} async-done(((f32[128,128,128]{2,1,0:T(8,128)}), f32[4,128,128]{2,1,0:T(8,128)}) %reduce-scatter.2.cloned.1.call-update) | async-done | bytes 262160 | tf_op jit(solution)/shard_map/reduce_scatter | solution.py:113
  524.9 2.5 scatter_fusion.3
  527.4 2.1 convert_element_type.38
  529.5 4.3 all-to-all-start.3
  534.4 64.7 %all-reduce.5.cloned.1.call-done = f32[1024,512]{1,0:T(8,128)} async-done(((f32[1024,512]{1,0:T(8,128)}), f32[1024,512]{1,0:T(8,128)}) %all-reduce.5.cloned.1.call-update) | async-done | bytes 2097168 | tf_op jit(solution)/shard_map/psum | solution.py:10
  599.1 3.1 broadcast_multiply_fusion
  (209 shorter events, 80.9 us)
Async XLA Ops:
  7.2 133.8 %copy-start = (bf16[1024,512]{1,0:T(8,128)(2,1)S(1)}, bf16[1024,512]{1,0:T(8,128)(2,1)}, u32[]{:S(2)}) copy-start(bf16[1024,512]{1,0:T(8,128)(2,1)} %param.16) | copy-start | bytes 3145732
  7.2 6.6 %copy-start.3 = (s32[32,32,2]{1,2,0:T(2,128)S(1)}, s32[32,32,2]{1,2,0:T(2,128)}, u32[]{:S(2)}) copy-start(s32[32,32,2]{1,2,0:T(2,128)} %param.23) | copy-start | bytes 24580
  7.2 6.8 %copy-start.8 = (s32[1,32,2]{1,2,0:T(2,128)S(1)}, s32[1,32,2]{1,2,0:T(2,128)}, u32[]{:S(2)}) copy-start(s32[1,32,2]{1,2,0:T(2,128)} %param.25) | copy-start | bytes 772
  7.2 7.4 %copy-start.4 = (s32[1,16,16]{2,1,0:T(8,128)S(1)}, s32[1,16,16]{2,1,0:T(8,128)}, u32[]{:S(2)}) copy-start(s32[1,16,16]{2,1,0:T(8,128)} %param.21) | copy-start | bytes 3076
  7.2 7.4 %copy-start.5 = (s32[1,16,16]{2,1,0:T(8,128)S(1)}, s32[1,16,16]{2,1,0:T(8,128)}, u32[]{:S(2)}) copy-start(s32[1,16,16]{2,1,0:T(8,128)} %param.20) | copy-start | bytes 3076
  7.2 7.5 %copy-start.6 = (s32[1,32,2]{1,2,0:T(2,128)S(1)}, s32[1,32,2]{1,2,0:T(2,128)}, u32[]{:S(2)}) copy-start(s32[1,32,2]{1,2,0:T(2,128)} %param.24) | copy-start | bytes 772
  7.2 7.7 %copy-start.1 = (bf16[16,128,128]{2,1,0:T(8,128)(2,1)S(1)}, bf16[16,128,128]{2,1,0:T(8,128)(2,1)}, u32[]{:S(2)}) copy-start(bf16[16,128,128]{2,1,0:T(8,128)(2,1)} %param.19) | copy-start | bytes 1572868
  9.3 14.9 %all-to-all-start = ((bf16[256,8,128]{2,0,1:T(8,128)(2,1)}), bf16[256,8,128]{2,0,1:T(8,128)(2,1)}, u32[]{:S(2)}, u32[]{:S(2)}) async-start(bf16[256,8,128]{2,0,1:T(8,128)(2,1)} %copy_bitcast_fusion.1), calls=%async_computation | async-start | bytes 1048576 | tf_op jit(solution)/shard_map/all_to_all | solution.py:37
  13.8 94.3 %all-gather.3.cloned.1.call-start = ((), (), s32[]{:S(2)}) async-start(), calls=%async_computation.8 | async-start | bytes 4325376 | tf_op jit(solution)/shard_map/all_gather | solution.py:65
  14.9 2.2 copy-start.9
  26.5 267.2 %all-reduce.3.cloned.1.call-start = ((), (), s32[]{:S(2)}) async-start(), calls=%async_computation.6 | async-start | bytes 4194304 | tf_op jit(solution)/shard_map/psum | solution.py:10
  126.0 15.0 %copy-start.7 = (f32[512]{0:T(512)S(1)}, f32[512]{0:T(512)}, u32[]{:S(2)}) copy-start(f32[512]{0:T(512)} %param.17) | copy-start | bytes 6148
  126.1 16.0 %copy-start.2 = (bf16[256,512]{1,0:T(8,128)(2,1)S(1)}, bf16[256,512]{1,0:T(8,128)(2,1)}, u32[]{:S(2)}) copy-start(bf16[256,512]{1,0:T(8,128)(2,1)} %param.18) | copy-start | bytes 786436
  145.6 13.8 %all-to-all-start.2 = ((bf16[256,8,128]{2,0,1:T(8,128)(2,1)}), bf16[256,8,128]{2,0,1:T(8,128)(2,1)S(1)}, u32[]{:S(2)}, u32[]{:S(2)}) async-start(bf16[256,8,128]{2,0,1:T(8,128)(2,1)} %bitcast.76), calls=%async_computation.2 | async-start | bytes 1048576 | tf_op jit(solution)/shard_map/all_to_all | solution.py:88
  149.1 375.8 %reduce-scatter.2.cloned.1.call-start = ((), (), s32[]{:S(2)}) async-start(), calls=%async_computation.5 | async-start | bytes 8650752 | tf_op jit(solution)/shard_map/reduce_scatter | solution.py:113
  184.5 414.6 %all-reduce.5.cloned.1.call-start = ((), (), s32[]{:S(2)}) async-start(), calls=%async_computation.7 | async-start | bytes 4194304 | tf_op jit(solution)/shard_map/psum | solution.py:10
  529.5 72.8 %all-to-all-start.3 = ((bf16[8,256,128]{2,1,0:T(8,128)(2,1)}), bf16[8,256,128]{2,1,0:T(8,128)(2,1)S(1)}, u32[]{:S(2)}, u32[]{:S(2)}) async-start(bf16[8,256,128]{2,1,0:T(8,128)(2,1)} %bitcast.26), calls=%async_computation.4 | async-start | bytes 1048576 | tf_op jit(solution)/shard_map/all_to_all | solution.py:116
Sparse Core Ops, SparseCore 0:
  26.6 81.3 all-gather.2
  144.2 149.4 all-reduce.2
  298.3 226.5 reduce-scatter.1
  527.1 71.9 all-reduce.4
